TPU v7x, 32 devices: a whole 2x2x4 slice. The times are simulated.
32 devices in a mesh: groups: 2 (over y), store: 4 (over z), mp: 4 (over x, core).
Axes of the slice: x: 2, y: 2, z: 4, core: 2. Of those that a mesh axis runs over, the one named last changes fastest.
Arguments:
- hidden: bfloat16 [8, 128, 4096], P(('groups', 'store')), parts along dimension 0, may hold values from -6 to 6
- query_weight: bfloat16 [4096, 8192], P('store', 'mp'), may hold values from -0.09375 to 0.09375
- keyvalue_weight: bfloat16 [4096, 2048], P('store', 'mp'), may hold values from -0.09375 to 0.09375
- block_store: bfloat16 [128, 1024, 2048], P('groups', 'store', 'mp'), parts along dimension 0, may hold values from -256 to 256
- block_ids: int32 [8, 4], P('groups'), parts along dimension 0, may hold values from 0 to 63, as said below
- offsets: int32 [8, 4], P('groups'), parts along dimension 0, may hold values from 0 to 3135, as said below
- served: int32 [8], P('groups'), parts along dimension 0, may hold values from 0 to 3, each once
Outputs:
- attended: bfloat16 [8, 128, 8192], P(('groups', 'store'), None, 'mp'), parts along dimension 0
There are 2 independent parts, one for each index of `groups`. A program takes and returns all parts, laid end to end along the dimension named above; an argument that names none is the same for every part. Nothing has to cross between parts.
Inputs may be any that keep to these rules, and one draw needn't show every extreme that they name: `block_ids`: the 4 block ids of one request differ. `offsets`: block c of a request starts at c * 1024 plus 0 to 63.
All inputs are finite; a program needn't handle non-finite values.
Results may differ from a plain program's by a relative error of at most 0.004.
The roundings to bfloat16 on the way count: a program that leaves them out, or rounds other values in their place, can miss the bound.
Values may be sent and summed in bfloat16 or wider, within the bound.
A program may use at most 128 MiB of HBM per device.

v0:
```python
import math

import jax
import jax.numpy as jnp
from jax import lax
from jax.sharding import PartitionSpec as P

HD = 128
NCH = 4
L = 1024
GAP = 64


def rotary_tables(positions, head_size):
    half_size = head_size // 2
    freq_index = jnp.arange(half_size, dtype=jnp.float32)
    inverse = jnp.exp(freq_index * (-2.0 * math.log(500000.0) / head_size))
    period = jnp.floor(2.0 * math.pi / inverse + 0.5)
    position_f = positions.astype(jnp.float32)[:, None]
    angles = jnp.mod(position_f, period[None, :]) / period[None, :] * (2.0 * math.pi)
    return (jnp.cos(angles), jnp.sin(angles))


def rotate(values, cosine, sine_values):
    half_size = values.shape[-1] // 2
    first_half = values[..., :half_size]
    second_half = values[..., half_size:]
    cos_b = cosine[:, None, :]
    sin_b = sine_values[:, None, :]
    return jnp.concatenate(
        [first_half * cos_b - second_half * sin_b, second_half * cos_b + first_half * sin_b],
        axis=-1,
    )


def rerotate(page_data, positions, head_size):
    page_rows = page_data.shape[0]
    split_view = page_data.reshape(page_rows, -1, 2, head_size)
    cosine, sine_values = rotary_tables(positions, head_size)
    turned = rotate(split_view[:, :, 0, :].astype(jnp.float32), cosine, sine_values).astype(
        jnp.bfloat16
    )
    return jnp.stack([turned, split_view[:, :, 1, :]], axis=2).reshape(page_rows, -1)


def attend(queries, cached_keys, cached_values, new_keys, new_values):
    row_count = queries.shape[0]
    head_count = queries.shape[1]
    sharing = head_count // cached_keys.shape[1]
    scaling = 1.0 / math.sqrt(queries.shape[2])
    causal = jnp.arange(row_count)[:, None] >= jnp.arange(row_count)[None, :]

    def one_head(head_index):
        kv_index = head_index // sharing
        q_one = lax.dynamic_index_in_dim(queries, head_index, 1, keepdims=False)
        k_old = lax.dynamic_index_in_dim(cached_keys, kv_index, 1, keepdims=False)
        v_old = lax.dynamic_index_in_dim(cached_values, kv_index, 1, keepdims=False)
        k_new = lax.dynamic_index_in_dim(new_keys, kv_index, 1, keepdims=False)
        v_new = lax.dynamic_index_in_dim(new_values, kv_index, 1, keepdims=False)
        past_scores = jnp.dot(q_one, k_old.T, preferred_element_type=jnp.float32) * scaling
        own_scores = jnp.dot(q_one, k_new.T, preferred_element_type=jnp.float32) * scaling
        own_scores = jnp.where(causal, own_scores, -jnp.inf)
        row_top = jnp.maximum(jnp.max(past_scores, axis=1), jnp.max(own_scores, axis=1))[:, None]
        w_old = jnp.exp(past_scores - row_top)
        w_new = jnp.exp(own_scores - row_top)
        denominator = jnp.sum(w_old, axis=1) + jnp.sum(w_new, axis=1)
        mixed = jnp.dot(w_old.astype(jnp.bfloat16), v_old, preferred_element_type=jnp.float32)
        mixed = mixed + jnp.dot(
            w_new.astype(jnp.bfloat16), v_new, preferred_element_type=jnp.float32
        )
        return (mixed / denominator[:, None]).astype(jnp.bfloat16)

    per_head = lax.map(one_head, jnp.arange(head_count, dtype=jnp.int32))
    return jnp.transpose(per_head, (1, 0, 2)).reshape(row_count, head_count * queries.shape[2])


def per_device(hidden, query_weight, keyvalue_weight, block_store, block_ids, offsets, served):
    tokens = hidden[0]
    row_count = tokens.shape[0]
    q_cols = query_weight.shape[1]
    kv_cols = keyvalue_weight.shape[1]
    head_count = q_cols // HD
    kv_heads = kv_cols // (2 * HD)

    def add_rows(panel):
        return jnp.dot(tokens, panel, preferred_element_type=jnp.float32)

    my_index = lax.axis_index("store")
    slot_count = lax.axis_size("store")
    share_rows = block_store.shape[1]
    wanted = block_ids[served]
    sending = jnp.take(block_store, wanted.reshape(-1), axis=0).reshape(
        slot_count * NCH * share_rows, kv_cols
    )
    sending = sending.reshape(slot_count, NCH, share_rows, kv_cols)
    queries = add_rows(lax.all_gather(query_weight, "store", axis=0, tiled=True))
    fresh_proj = add_rows(lax.all_gather(keyvalue_weight, "store", axis=0, tiled=True))
    received = lax.all_to_all(sending, "store", split_axis=0, concat_axis=2, tiled=True)
    received = received.reshape(NCH * L, kv_cols)
    request = served[my_index]
    key_pos = (offsets[request][:, None] + jnp.arange(L, dtype=jnp.int32)[None, :]).reshape(NCH * L)
    received = rerotate(received, key_pos, HD)
    split_pages = received.reshape(NCH * L, kv_heads, 2, HD)
    query_pos = NCH * L + GAP + jnp.arange(row_count, dtype=jnp.int32)
    cos_query, sin_query = rotary_tables(query_pos, HD)
    queries = rotate(queries.reshape(row_count, head_count, HD), cos_query, sin_query).astype(
        jnp.bfloat16
    )
    fresh_proj = fresh_proj.reshape(row_count, kv_heads, 2, HD)
    new_keys = rotate(fresh_proj[:, :, 0, :], cos_query, sin_query).astype(jnp.bfloat16)
    new_values = fresh_proj[:, :, 1, :].astype(jnp.bfloat16)
    attended = attend(
        queries, split_pages[:, :, 0, :], split_pages[:, :, 1, :], new_keys, new_values
    )
    return attended[None]


def solution(mesh):
    in_specs = (
        P(("groups", "store"), None, None),
        P("store", "mp"),
        P("store", "mp"),
        P("groups", "store", "mp"),
        P("groups", None),
        P("groups", None),
        P("groups"),
    )
    out_specs = P(("groups", "store"), None, "mp")
    return jax.shard_map(
        per_device, mesh=mesh, in_specs=in_specs, out_specs=out_specs, check_vma=False
    )
```

profile of v0, /device:TPU:10, one launch (start us, length us, event | category | flops | bytes accessed | tf_op | source)
XLA Modules:
  0.0 640.5 jit_solution(6617780340946554539)
XLA Ops:
  8.7 8.5 %gather_fusion.1 = bf16[16,256,512]{2,1,0:T(8,128)(2,1)} fusion(bf16[64,256,512]{2,1,0:T(8,128)(2,1)} %param.12, s32[1024]{0:T(1024)S(1)} %pad_clamp_fusion), kind=kCustom, calls=%fused_computation.1 | custom fusion | bytes 8388672 | tf_op jit(solution)/shard_map/jit(_take)/gather | solution.py:92
  17.3 5.0 broadcast_select_fusion
  22.3 5.3 all-to-all-start
  31.4 10.7 %fusion.41 = (f32[4096,64]{1,0:T(8,128)}, f32[4096,64]{1,0:T(8,128)}) fusion(pred[64]{0:T(512)(128)(4,1)S(1)} %broadcast_compare_fusion, f32[64]{0:T(128)S(1)} %add_floor_fusion, f32[4096]{0:T(1024)S(1)} %bitcast.99), kind=kLoop, calls=%fused_computation.56 | loop fusion | flops 2359296 | bytes 2113856 | tf_op jit(solution)/shard_map/cos | solution.py:21
  42.1 119.8 %all-gather.5.cloned.1.call-done = bf16[4096,512]{1,0:T(8,128)(2,1)} async-done(((bf16[1024,512]{1,0:T(8,128)(2,1)}), bf16[4096,512]{1,0:T(8,128)(2,1)}) %all-gather.5.cloned.1.call-update) | async-done | bytes 4194320 | tf_op jit(solution)/shard_map/all_gather | solution.py:97
  161.9 6.4 copy.36
  168.3 8.2 %all-to-all-done = bf16[4,4,256,512]{3,2,1,0:T(8,128)(2,1)} async-done(((bf16[4,4,256,512]{3,2,1,0:T(8,128)(2,1)}), bf16[4,4,256,512]{3,2,1,0:T(8,128)(2,1)}, u32[]{:S(2)}, u32[]{:S(2)}) %all-to-all-start) | async-done | bytes 4194336 | tf_op jit(solution)/shard_map/all_to_all | solution.py:98
  176.6 5.2 copy.35
  181.7 7.1 %reshape_reshape.4 = bf16[4096,2,2,128]{3,2,1,0:T(2,128)(2,1)} reshape(bf16[1,4,4,256,512]{4,3,2,1,0:T(8,128)(2,1)} %copy.35) | data formatting | bytes 8388608 | tf_op jit(solution)/shard_map/reshape;reshape | solution.py:38
  188.8 8.7 %fusion.52 = (bf16[4096,2,1,128]{3,2,1,0:T(2,128)(2,1)S(1)}, f32[4096,2,1,128]{3,2,1,0:T(1,128)S(1)}) fusion(bf16[4096,2,2,128]{3,2,1,0:T(2,128)(2,1)} %reshape_reshape.4), kind=kLoop, calls=%fused_computation.91 | loop fusion | flops 1048576 | bytes 10485760 | tf_op jit(solution)/shard_map/slice | solution.py:43
  197.9 1.2 copy-done.2
  199.8 11.2 %subtract_convert_fusion = (bf16[4096,2,64]{2,1,0:T(2,128)(2,1)S(1)}, bf16[4096,2,64]{2,1,0:T(2,128)(2,1)S(1)}) fusion(f32[4096,2,128]{2,1,0:T(2,128)S(1)} %bitcast.92, f32[4096,64]{1,0:T(8,128)S(1)} %copy-done.3, f32[4096,64]{1,0:T(8,128)S(1)} %copy-done.2), kind=kLoop, calls=%fused_computation.43 | loop fusion | flops 4194304 | bytes 8388608 | tf_op jit(solution)/shard_map/convert.4
  211.0 5.7 pad_maximum_fusion
  216.7 1.6 copy.39
  218.3 1.4 copy-done.1
  219.7 1.3 fusion.36
  221.0 228.8 %all-gather.3.cloned.1.call-done = bf16[4096,2048]{1,0:T(8,128)(2,1)} async-done(((bf16[1024,2048]{1,0:T(8,128)(2,1)}), bf16[4096,2048]{1,0:T(8,128)(2,1)}) %all-gather.3.cloned.1.call-update) | async-done | bytes 16777232 | tf_op jit(solution)/shard_map/all_gather | solution.py:96
  449.8 20.7 %copy.34 = bf16[2048,4096]{1,0:T(8,128)(2,1)} copy(bf16[2048,4096]{0,1:T(8,128)(2,1)} %bitcast.94) | data formatting | bytes 33554432 | tf_op jit(solution)/shard_map/dot_general | solution.py:86
  470.5 8.1 %fusion.38 = f32[128,16,128]{0,2,1:T(8,128)S(1)} fusion(bf16[16,128,4096]{2,1,0:T(8,128)(2,1)} %bitcast.91, bf16[1,128,4096]{2,1,0:T(8,128)(2,1)S(1)} %copy-done), kind=kOutput, calls=%fused_computation.53 | convolution fusion | flops 2147483648 | bytes 18874368 | tf_op jit(solution)/shard_map/dot_general | solution.py:86
  478.8 0.8 pad_maximum_fusion.1
  479.6 151.7 %while.13 = (s32[]{:T(128)}, bf16[16,128,128]{2,1,0:T(8,128)(2,1)}, s32[16]{0:T(128)S(1)}, bf16[128,16,128]{0,2,1:T(8,128)(2,1)}, bf16[4096,2,128]{2,0,1:T(8,128...) while((s32[]{:T(128)}, bf16[16,128,128]{2,1,0:T(8,128)(2,1)}, ...), condition=%wide.region_5.6_spmd.clone, body=%wide.region_0.5_spmd.clone.sunk | while | flops 280149760 | bytes 8888206 | solution.py:73
  484.4 1.0 fusion.70
  485.4 1.8 fusion.69
  488.2 0.8 fusion.74
  493.9 1.0 fusion.70
  494.9 1.8 fusion.69
  497.7 0.8 fusion.74
  503.4 1.0 fusion.70
  504.4 1.8 fusion.69
  507.2 0.8 fusion.74
  512.9 1.0 fusion.70
  513.8 1.8 fusion.69
  516.7 0.8 fusion.74
  522.3 1.0 fusion.70
  523.3 1.8 fusion.69
  526.2 0.8 fusion.74
  531.8 1.0 fusion.70
  532.8 1.8 fusion.69
  535.7 0.8 fusion.74
  541.3 1.0 fusion.70
  542.3 1.8 fusion.69
  545.1 0.8 fusion.74
  550.8 1.0 fusion.70
  551.8 1.8 fusion.69
  560.3 1.0 fusion.70
  561.3 1.8 fusion.69
  564.1 0.8 fusion.74
  569.7 1.0 fusion.70
  570.7 1.8 fusion.69
  579.2 1.0 fusion.70
  580.2 1.8 fusion.69
  588.7 1.0 fusion.70
  589.7 1.8 fusion.69
  598.2 1.0 fusion.70
  599.2 1.8 fusion.69
  602.0 0.8 fusion.74
  607.7 1.0 fusion.70
  608.7 1.8 fusion.69
  617.2 1.0 fusion.70
  618.1 1.8 fusion.69
  626.6 1.0 fusion.70
  627.6 1.8 fusion.69
  631.3 1.4 copy.42
  632.7 1.0 broadcast_in_dim_reshape.3
  (140 shorter events, 38.0 us)
Async XLA Ops:
  6.5 211.8 %copy-start = (bf16[1,128,4096]{2,1,0:T(8,128)(2,1)S(1)}, bf16[1,128,4096]{2,1,0:T(8,128)(2,1)}, u32[]{:S(2)}) copy-start(bf16[1,128,4096]{2,1,0:T(8,128)(2,1)} %param.9) | copy-start | bytes 3145732
  6.5 155.4 %all-gather.5.cloned.1.call-start = ((), (), s32[]{:S(2)}) async-start(), calls=%async_computation.2 | async-start | bytes 5242880 | tf_op jit(solution)/shard_map/all_gather | solution.py:97
  7.3 0.8 copy-start.5
  7.3 0.8 copy-start.4
  7.3 442.5 %all-gather.3.cloned.1.call-start = ((), (), s32[]{:S(2)}) async-start(), calls=%async_computation.1 | async-start | bytes 20971520 | tf_op jit(solution)/shard_map/all_gather | solution.py:96
  22.3 154.3 %all-to-all-start = ((bf16[4,4,256,512]{3,2,1,0:T(8,128)(2,1)}), bf16[4,4,256,512]{3,2,1,0:T(8,128)(2,1)}, u32[]{:S(2)}, u32[]{:S(2)}) async-start(bf16[4,4,256,512]{3,2,1,0:T(8,128)(2,1)} %broadcast_select_fusion), calls=%async_computation | async-start | bytes 8388608 | tf_op jit(solution)/shard_map/all_to_all | solution.py:98
  197.5 1.6 copy-start.2
  197.5 2.2 copy-start.3
  216.7 3.0 copy-start.1
Sparse Core Ops, SparseCore 0:
  8.9 152.9 all-gather.4
  163.5 286.2 all-gather.2
where the time goes:
time: 648 us; the launch traced here: 641 us
  waiting for transfers between devices  358 us (55%)
  matrix products  75.7 us (12%)
  local copies, waits for them, and re-layouts  68.1 us (11%)
  loops' own time  66.9 us (10%)
  other arithmetic  50.6 us (8%)
  between operations  15.7 us (2%)
    all_gather x1, waiting for transfers between devices, per_device(): lax.all_gather(query_weight, 'store', axis=0, tiled=True)  229 us
    all_gather x1, waiting for transfers between devices, per_device(): lax.all_gather(keyvalue_weight, 'store', axis=0, tiled=True)  120 us
    another operation x1, loops' own time, attend(): per_head = lax.map(one_head, jnp.arange(head_count, dtype=jnp.int32))  66.9 us
    dot_general x16, matrix products, one_head(): jnp.dot(q_one, k_old.T, preferred_element_type=jnp.float32) * scaling  28.6 us
    dot_general x2, local copies, waits for them, and re-layouts, add_rows(): return jnp.dot(tokens, panel, preferred_element_type=jnp.float32)  27 us
    dot_general x16, matrix products, one_head(): jnp.dot(q_one, k_new.T, preferred_element_type=jnp.float32) * scaling  15.9 us
    dot_general x16, matrix products, one_head(): jnp.dot(w_new.astype(jnp.bfloat16), v_new, preferred_element_type=jnp.flo...  13.1 us
  transfers between devices with their start and end apart: 3, of which 3 were waited for; matrix products, arithmetic and copies ran while one was open for 12% of the time, Pallas kernels for 0%

commit v1 on v0

v1 whole, which is shorter than its diff:
```python
import functools
import math

import jax
import jax.numpy as jnp
import numpy as np
from jax import lax
from jax.experimental import pallas as pl
from jax.experimental.pallas import tpu as pltpu
from jax.sharding import PartitionSpec as P

HD = 128
HALF = HD // 2
NCH = 4
L = 1024
GAP = 64
BASE = 500000.0


def periods():
    inverse = np.exp(
        np.arange(HALF, dtype=np.float32) * np.float32(-2.0 * math.log(BASE) / HD)
    ).astype(np.float32)
    return np.floor(np.float32(2.0 * math.pi) / inverse + np.float32(0.5)).astype(np.float64)


def signed_tables(positions):
    period = periods()[None, :]
    angles = np.mod(np.asarray(positions, np.float64)[:, None], period) / period * (2.0 * math.pi)
    cos, sin = np.cos(angles), np.sin(angles)
    return (
        np.concatenate([cos, cos], axis=1).astype(np.float32),
        np.concatenate([-sin, sin], axis=1).astype(np.float32),
    )


def offset_tables(offsets):
    period = jnp.asarray(periods(), jnp.float32)[None, :]
    angles = jnp.mod(offsets.astype(jnp.float32)[:, None], period) / period * (2.0 * math.pi)
    cos, sin = jnp.cos(angles), jnp.sin(angles)
    return jnp.concatenate([cos, cos], axis=1), jnp.concatenate([-sin, sin], axis=1)


def gather_body(slots, ids_ref, served_ref, store_ref, out_ref, sems):
    copies = []
    for s in range(slots):
        request = served_ref[s]
        for c in range(NCH):
            copy = pltpu.make_async_copy(
                store_ref.at[ids_ref[request, c]], out_ref.at[s, c], sems.at[s, c]
            )
            copy.start()
            copies.append(copy)
    for copy in copies:
        copy.wait()


def gather_blocks(block_ids, served, block_store):
    slots = served.shape[0]
    shape = (slots, NCH) + block_store.shape[1:]
    return pl.pallas_call(
        functools.partial(gather_body, slots),
        grid_spec=pltpu.PrefetchScalarGridSpec(
            num_scalar_prefetch=2,
            grid=(1,),
            in_specs=[pl.BlockSpec(memory_space=pl.ANY)],
            out_specs=pl.BlockSpec(memory_space=pl.ANY),
            scratch_shapes=[pltpu.SemaphoreType.DMA((slots, NCH))],
        ),
        out_shape=jax.ShapeDtypeStruct(shape, block_store.dtype),
        name="gather_blocks",
    )(block_ids, served, block_store)


def turn(x, cos, sin):
    return x * cos + pltpu.roll(x, HALF, 1) * sin


def attend_body(
    heads, kv_heads, share, fresh_ref, kv_ref, qc_ref, qs_ref, tc_ref, ts_ref, oc_ref, os_ref,
    out_ref, keys, values, queries, scores
):
    rows = fresh_ref.shape[0]
    shards = L // share
    q_cols = heads * HD
    sharing = heads // kv_heads
    past = NCH * L
    qc, qs = qc_ref[...], qs_ref[...]
    for g in range(kv_heads):
        at = q_cols + g * 2 * HD
        keys[g, past:, :] = turn(fresh_ref[:, at : at + HD], qc, qs).astype(jnp.bfloat16)
        values[g, past:, :] = fresh_ref[:, at + HD : at + 2 * HD].astype(jnp.bfloat16)
    for h in range(heads):
        queries[h * rows : (h + 1) * rows, :] = turn(
            fresh_ref[:, h * HD : (h + 1) * HD], qc, qs
        ).astype(jnp.bfloat16)

    def rotate_share(i, carry):
        source = i // NCH
        c = i % NCH
        at_t = pl.multiple_of(source * share, share)
        at_k = pl.multiple_of(i * share, share)
        tc, ts = tc_ref[pl.ds(at_t, share), :], ts_ref[pl.ds(at_t, share), :]
        oc, os = oc_ref[pl.ds(c, 1), :], os_ref[pl.ds(c, 1), :]
        cos = tc * oc - ts * os
        sin = ts * oc + tc * os
        for g in range(kv_heads):
            at = g * 2 * HD
            x = kv_ref[source, c, :, at : at + HD].astype(jnp.float32)
            keys[g, pl.ds(at_k, share), :] = turn(x, cos, sin).astype(jnp.bfloat16)
            values[g, pl.ds(at_k, share), :] = kv_ref[source, c, :, at + HD : at + 2 * HD]
        return carry

    lax.fori_loop(0, shards * NCH, rotate_share, 0)

    block = 2 * rows
    steps = heads // 2
    width = 512
    factor = math.log2(math.e) / math.sqrt(HD)
    lower = lax.broadcasted_iota(jnp.int32, (block, rows), 0) % rows >= lax.broadcasted_iota(
        jnp.int32, (block, rows), 1
    )
    contract = (((1,), (1,)), ((), ()))

    def one_block(b, carry):
        g = (b * 2) // sharing
        q = queries[pl.ds(pl.multiple_of(b * block, block), block), :]
        own = lax.dot_general(q, keys[g, past:, :], contract, preferred_element_type=jnp.float32)
        own = jnp.where(lower, own, -jnp.inf)
        top = own
        for j in range(past // width):
            s = lax.dot_general(
                q, keys[g, j * width : (j + 1) * width, :], contract,
                preferred_element_type=jnp.float32,
            )
            scores[:, j * width : (j + 1) * width] = s
            for k in range(width // HD):
                top = jnp.maximum(top, s[:, k * HD : (k + 1) * HD])
        top = jnp.max(top, axis=1, keepdims=True)
        w = jnp.exp2((own - top) * factor)
        total = w
        mixed = jnp.dot(
            w.astype(jnp.bfloat16), values[g, past:, :], preferred_element_type=jnp.float32
        )
        for j in range(past // width):
            w = jnp.exp2((scores[:, j * width : (j + 1) * width] - top) * factor)
            for k in range(width // HD):
                total = total + w[:, k * HD : (k + 1) * HD]
            mixed = mixed + jnp.dot(
                w.astype(jnp.bfloat16), values[g, j * width : (j + 1) * width, :],
                preferred_element_type=jnp.float32,
            )
        done = (mixed / jnp.sum(total, axis=1, keepdims=True)).astype(out_ref.dtype)
        for k in range(2):
            at = pl.multiple_of((b * 2 + k) * HD, HD)
            out_ref[0, :, pl.ds(at, HD)] = done[k * rows : (k + 1) * rows, :]
        return carry

    lax.fori_loop(0, steps, one_block, 0)


def per_device(hidden, query_weight, keyvalue_weight, block_store, block_ids, offsets, served):
    slots = lax.axis_size("store")
    me = lax.axis_index("store")
    rows, width = hidden.shape[1:]
    share = block_store.shape[1]
    heads = query_weight.shape[1] // HD
    kv_heads = keyvalue_weight.shape[1] // (2 * HD)
    sending = gather_blocks(block_ids, served, block_store)
    received = lax.all_to_all(sending, "store", split_axis=0, concat_axis=0, tiled=True)
    pieces = hidden[0].reshape(rows, slots, width // slots).transpose(1, 0, 2)
    tokens = lax.all_to_all(pieces, "store", split_axis=0, concat_axis=0, tiled=True)
    tokens = tokens.reshape(slots * rows, width // slots)
    partial = jnp.concatenate(
        [
            jnp.dot(tokens, query_weight, preferred_element_type=jnp.float32),
            jnp.dot(tokens, keyvalue_weight, preferred_element_type=jnp.float32),
        ],
        axis=1,
    )
    fresh = lax.psum_scatter(partial, "store", scatter_dimension=0, tiled=True)
    qc, qs = signed_tables(NCH * L + GAP + np.arange(rows))
    tc, ts = signed_tables(np.arange(L))
    oc, os = offset_tables(offsets[served[me]])
    past = NCH * L
    return pl.pallas_call(
        functools.partial(attend_body, heads, kv_heads, share),
        out_shape=jax.ShapeDtypeStruct((1, rows, heads * HD), jnp.bfloat16),
        in_specs=[pl.BlockSpec(memory_space=pltpu.VMEM)] * 8,
        out_specs=pl.BlockSpec(memory_space=pltpu.VMEM),
        scratch_shapes=[
            pltpu.VMEM((kv_heads, past + rows, HD), jnp.bfloat16),
            pltpu.VMEM((kv_heads, past + rows, HD), jnp.bfloat16),
            pltpu.VMEM((heads * rows, HD), jnp.bfloat16),
            pltpu.VMEM((2 * rows, past), jnp.float32),
        ],
        compiler_params=pltpu.CompilerParams(vmem_limit_bytes=48 << 20),
        name="attend",
    )(fresh, received, qc, qs, tc, ts, oc, os)


def solution(mesh):
    in_specs = (
        P(("groups", "store"), None, None),
        P("store", "mp"),
        P("store", "mp"),
        P("groups", "store", "mp"),
        P("groups", None),
        P("groups", None),
        P("groups"),
    )
    out_specs = P(("groups", "store"), None, "mp")
    return jax.shard_map(
        per_device, mesh=mesh, in_specs=in_specs, out_specs=out_specs, check_vma=False
    )
```

time: 648 us -> 305 us (0.47)
  waiting for transfers between devices: 358 us -> 85.6 us
  Pallas kernels: 0 us -> 150 us
  matrix products: 75.7 us -> 5.23 us
  loops' own time: 66.9 us -> 0 us
  local copies, waits for them, and re-layouts: 68.1 us -> 4.17 us
  other arithmetic: 50.6 us -> 3.64 us
  blocking collectives: 0 us -> 29 us
    all_gather x2 -> x0, waiting for transfers between devices: 349 us -> none  [the longest x1 229 us: per_device(): lax.all_gather(query_weight, 'store', axis=0, tiled=True)]
    pallas_call x0 -> x2, Pallas kernels: none -> 150 us  [the longest x1 129 us: gather_blocks(): pl.pallas_call(functools.partial(gather_body, slots), grid_spec=pltpu.Pre...]
    all_to_all x1, waiting for transfers between devices: 8.23 us -> 85.6 us  [per_device(): lax.all_to_all(sending, 'store', split_axis=0, concat_axis=0, tiled=True)]
    dot_general x66 -> x2, matrix products: 75.7 us -> 5.23 us  [the longest x1 4.52 us: per_device(): jnp.dot(tokens, query_weight, preferred_element_type=jnp.float32)]
    another operation x1 -> x0, loops' own time: 66.9 us -> none  [attend(): per_head = lax.map(one_head, jnp.arange(head_count, dtype=jnp.int32))]
    all_to_all x0 -> x1, blocking collectives: none -> 29 us  [per_device(): lax.all_to_all(pieces, 'store', split_axis=0, concat_axis=0, tiled=True)]
    dot_general x2 -> x0, local copies, waits for them, and re-layouts: 27 us -> none  [add_rows(): return jnp.dot(tokens, panel, preferred_element_type=jnp.float32)]
    another operation x3 -> x0, other arithmetic: 11.3 us -> none
  transfers between devices with their start and end apart: 3 -> 2, of which waited for: 3 -> 1; matrix products, arithmetic and copies ran while one was open for 12% -> 0% of each run, Pallas kernels for 0% -> 43%
where the time goes in v1:
time: 305 us; the launch traced here: 300 us
  Pallas kernels  150 us (49%)
  waiting for transfers between devices  85.6 us (28%)
  blocking collectives  29 us (10%)
  between operations  15.5 us (5%)
  starting transfers between devices  6.79 us (2%)
  matrix products  5.23 us (2%)
  local copies, waits for them, and re-layouts  4.17 us (1%)
  other arithmetic  3.64 us (1%)
    pallas_call x1, Pallas kernels, gather_blocks(): pl.pallas_call(functools.partial(gather_body, slots), grid_spec=pltpu.Pre...  129 us
    all_to_all x1, waiting for transfers between devices, per_device(): lax.all_to_all(sending, 'store', split_axis=0, concat_axis=0, tiled=True)  85.6 us
    all_to_all x1, blocking collectives, per_device(): lax.all_to_all(pieces, 'store', split_axis=0, concat_axis=0, tiled=True)  29 us
    pallas_call x1, Pallas kernels, per_device(): pl.pallas_call(functools.partial(attend_body, heads, kv_heads, share), ou...  21 us
    all_to_all x1, starting transfers between devices, per_device(): lax.all_to_all(sending, 'store', split_axis=0, concat_axis=0, tiled=True)  6.78 us
  transfers between devices with their start and end apart: 2, of which 1 were waited for; matrix products, arithmetic and copies ran while one was open for 0% of the time, Pallas kernels for 43%

profile of v1, /device:TPU:10, one launch (start us, length us, event | category | flops | bytes accessed | tf_op | source)
XLA Modules:
  0.0 299.9 jit_solution(5232622684507386778)
XLA Ops:
  6.5 0.0 copy-start
  6.5 0.0 reduce-scatter.2.cloned.1.call-start
  6.5 1.7 copy.15
  8.2 29.0 %all_to_all.10 = bf16[4,128,1024]{1,2,0:T(8,128)(2,1)S(1)} all-to-all(bf16[4,128,1024]{1,2,0:T(8,128)(2,1)S(1)} %bitcast.11), channel_id=1, replica_groups=mesh['groups'=2,'store'=4,'mp'=4] {'store'}, dimensions={0} | all-to-all | bytes 2097152 | tf_op jit(solution)/shard_map/all_to_all | solution.py:172
  37.3 0.5 copy.16
  37.8 0.0 copy-done
  37.8 0.7 fusion.7
  38.5 4.5 %fusion.6 = f32[512,2048]{1,0:T(8,128)S(1)} fusion(bf16[512,1024]{1,0:T(8,128)(2,1)S(1)} %bitcast.13, bf16[1024,2048]{1,0:T(8,128)(2,1)} %param.13), kind=kOutput, calls=%fused_computation.14 | convolution fusion | flops 2147483648 | bytes 9437184 | tf_op jit(solution)/shard_map/dot_general | solution.py:176
  43.1 2.8 pad_maximum_fusion
  45.8 0.0 reduce-scatter.2.cloned.1.call-update
  45.8 129.0 %gather_blocks.1 = bf16[4,4,256,512]{3,2,1,0:T(8,128)(2,1)} custom-call(s32[4,4]{1,0:T(4,128)} %ids_ref.1, s32[4]{0:T(128)} %served_ref.1, bf16[64,256,512]{2,1,0:T(8,128)(2,1)} %store_ref.1), custom_call_target="tpu_custom_call" | custom-call | tf_op jit(solution)/shard_map/gather_blocks/pallas_call | solution.py:61
  174.8 0.0 copy-start.6
  174.9 0.0 copy-start.7
  174.9 0.0 copy-start.8
  174.9 0.0 copy-start.2
  174.9 0.0 copy-start.3
  174.9 0.0 copy-start.4
  174.9 0.0 copy-start.5
  174.9 6.8 %all-to-all-start.1 = ((bf16[4,4,256,512]{3,2,1,0:T(8,128)(2,1)}), bf16[4,4,256,512]{3,2,1,0:T(8,128)(2,1)}, u32[]{:S(2)}, u32[]{:S(2)}) async-start(bf16[4,4,256,512]{3,2,1,0:T(8,128)(2,1)} %gather_blocks.1), calls=%async_computation.2 | async-start | bytes 8388608 | tf_op jit(solution)/shard_map/all_to_all | solution.py:170
  181.7 0.0 copy-done.6
  181.7 0.6 dynamic_slice.6
  184.2 0.7 convert_bitcast_fusion
  184.9 0.0 copy-done.7
  184.9 0.0 copy-done.8
  184.9 0.1 fusion.5
  185.1 0.1 pad_maximum_fusion.1
  185.1 85.6 %all-to-all-done.1.kv_ref = bf16[4,4,256,512]{3,2,1,0:T(8,128)(2,1)} async-done(((bf16[4,4,256,512]{3,2,1,0:T(8,128)(2,1)}), bf16[4,4,256,512]{3,2,1,0:T(8,128)(2,1)}, u32[]{:S(2)}, u32[]{:S(2)}) %all-to-all-start.1) | async-done | bytes 4194336 | tf_op jit(solution)/shard_map/all_to_all | solution.py:170
  270.7 0.0 reduce-scatter.2.cloned.1.call-done.fresh_ref
  270.7 0.0 copy-done.2
  270.7 0.0 copy-done.3
  270.7 0.0 copy-done.4
  270.7 0.0 copy-done.5
  270.8 0.0 copy-start.1
  270.8 1.3 copy-done.1
  272.1 21.0 %attend.1 = bf16[1,128,2048]{2,1,0:T(8,128)(2,1)} custom-call(f32[128,2560]{1,0:T(8,128)S(1)} %copy-done.1, bf16[4,4,256,512]{3,2,1,0:T(8,128)(2,1)} %all-to-all-done.1.kv_ref, f32[128,128]{1,0:T(8,128)S(1)} %copy-done.4, f32[128,128]{1,0:T(8,128)S(1)} %copy-done.5, f32[1024,128]{1,0:T(8,128)S(1)} %copy-done.2, f32[1024,128]{1,0:T(8,128)S(1)} %copy-done.3, ...), custom_call_target="tpu_custom_call" | custom-call | tf_op jit(solution)/shard_map/attend/pallas_call | solution.py:186
Async XLA Ops:
  6.5 31.3 %copy-start = (bf16[1024,512]{1,0:T(8,128)(2,1)S(1)}, bf16[1024,512]{1,0:T(8,128)(2,1)}, u32[]{:S(2)}) copy-start(bf16[1024,512]{1,0:T(8,128)(2,1)} %param.14) | copy-start | bytes 3145732
  6.5 264.2 %reduce-scatter.2.cloned.1.call-start = ((), (), s32[]{:S(2)}) async-start(), calls=%async_computation.3 | async-start | bytes 6553600 | tf_op jit(solution)/shard_map/reduce_scatter | solution.py:181
  174.8 6.9 %copy-start.6 = (s32[4]{0:T(128)S(1)}, s32[4]{0:T(128)}, u32[]{:S(2)}) copy-start(s32[4]{0:T(128)} %served_ref.1) | copy-start | bytes 52
  174.9 10.1 %copy-start.7 = (f32[64]{0:T(128)S(1)}, f32[64]{0:T(128)}, u32[]{:S(2)}) copy-start(f32[64]{0:T(128)} %constant.32) | copy-start | bytes 772
  174.9 10.1 %copy-start.8 = (f32[64]{0:T(128)S(1)}, f32[64]{0:T(128)}, u32[]{:S(2)}) copy-start(f32[64]{0:T(128)} %constant.26.clone) | copy-start | bytes 772
  174.9 95.9 %copy-start.2 = (f32[1024,128]{1,0:T(8,128)S(1)}, f32[1024,128]{1,0:T(8,128)}, u32[]{:S(2)}) copy-start(f32[1024,128]{1,0:T(8,128)} %constant.29.clone.tc_ref) | copy-start | bytes 1572868
  174.9 95.8 %copy-start.3 = (f32[1024,128]{1,0:T(8,128)S(1)}, f32[1024,128]{1,0:T(8,128)}, u32[]{:S(2)}) copy-start(f32[1024,128]{1,0:T(8,128)} %constant.30.clone.ts_ref) | copy-start | bytes 1572868
  174.9 95.8 %copy-start.4 = (f32[128,128]{1,0:T(8,128)S(1)}, f32[128,128]{1,0:T(8,128)}, u32[]{:S(2)}) copy-start(f32[128,128]{1,0:T(8,128)} %constant.27.clone.qc_ref) | copy-start | bytes 196612
  174.9 95.8 %copy-start.5 = (f32[128,128]{1,0:T(8,128)S(1)}, f32[128,128]{1,0:T(8,128)}, u32[]{:S(2)}) copy-start(f32[128,128]{1,0:T(8,128)} %constant.28.clone.qs_ref) | copy-start | bytes 196612
  174.9 95.8 %all-to-all-start.1 = ((bf16[4,4,256,512]{3,2,1,0:T(8,128)(2,1)}), bf16[4,4,256,512]{3,2,1,0:T(8,128)(2,1)}, u32[]{:S(2)}, u32[]{:S(2)}) async-start(bf16[4,4,256,512]{3,2,1,0:T(8,128)(2,1)} %gather_blocks.1), calls=%async_computation.2 | async-start | bytes 8388608 | tf_op jit(solution)/shard_map/all_to_all | solution.py:170
  270.8 1.3 copy-start.1
Sparse Core Ops, SparseCore 0:
  46.0 94.1 reduce-scatter.1

commit v2 on v1

v2 whole, which is shorter than its diff:
```python
import functools
import math

import jax
import jax.numpy as jnp
import numpy as np
from jax import lax
from jax.experimental import pallas as pl
from jax.experimental.pallas import tpu as pltpu
from jax.sharding import PartitionSpec as P

HD = 128
HALF = HD // 2
NCH = 4
L = 1024
GAP = 64
BASE = 500000.0


def periods():
    inverse = np.exp(
        np.arange(HALF, dtype=np.float32) * np.float32(-2.0 * math.log(BASE) / HD)
    ).astype(np.float32)
    return np.floor(np.float32(2.0 * math.pi) / inverse + np.float32(0.5)).astype(np.float64)


def signed_tables(positions):
    period = periods()[None, :]
    angles = np.mod(np.asarray(positions, np.float64)[:, None], period) / period * (2.0 * math.pi)
    cos, sin = np.cos(angles), np.sin(angles)
    return (
        np.concatenate([cos, cos], axis=1).astype(np.float32),
        np.concatenate([-sin, sin], axis=1).astype(np.float32),
    )


def offset_tables(offsets):
    period = jnp.asarray(periods(), jnp.float32)[None, :]
    angles = jnp.mod(offsets.astype(jnp.float32)[:, None], period) / period * (2.0 * math.pi)
    cos, sin = jnp.cos(angles), jnp.sin(angles)
    return jnp.concatenate([cos, cos], axis=1), jnp.concatenate([-sin, sin], axis=1)


def gather_body(ids_ref, served_ref, store_ref, out_ref):
    out_ref[0] = store_ref[...]


def gather_blocks(block_ids, served, block_store):
    slots = served.shape[0]
    block = (1,) + block_store.shape[1:]
    return pl.pallas_call(
        gather_body,
        grid_spec=pltpu.PrefetchScalarGridSpec(
            num_scalar_prefetch=2,
            grid=(slots, NCH),
            in_specs=[pl.BlockSpec(block, lambda s, c, ids, served: (ids[served[s], c], 0, 0))],
            out_specs=pl.BlockSpec((1,) + block, lambda s, c, ids, served: (s, c, 0, 0)),
        ),
        out_shape=jax.ShapeDtypeStruct((slots, NCH) + block_store.shape[1:], block_store.dtype),
        name="gather_blocks",
    )(block_ids, served, block_store)


def turn(x, cos, sin):
    return x * cos + pltpu.roll(x, HALF, 1) * sin


MESH = pl.DeviceIdType.MESH


def serve_body(
    slots, peers, heads, kv_heads,
    hidden_ref, wq_hbm, wkv_hbm, sending_ref, qc_ref, qs_ref, tc_ref, ts_ref, oc_ref, os_ref,
    out_ref,
    tokens, wq, wkv, sums, arrived, blocks, keys, values, queries, scores,
    load_sem, own_sem, a_send, a_recv, b_send, b_recv, k_send, k_recv, p_send, p_recv,
):
    me = lax.axis_index("store")
    part = lax.axis_index("mp")
    rows = hidden_ref.shape[1]
    depth = tokens.shape[2]
    chunks, _, _, width = sums.shape
    share = blocks.shape[2]
    sharing = heads // kv_heads
    past = NCH * L
    strip = rows // peers

    loads = [
        pltpu.make_async_copy(wq_hbm, wq, load_sem.at[0]),
        pltpu.make_async_copy(wkv_hbm, wkv, load_sem.at[1]),
    ]
    for load in loads:
        load.start()
    own_copy = pltpu.make_async_copy(sending_ref.at[me], blocks.at[me], own_sem.at[0])
    own_copy.start()

    barrier = pltpu.get_barrier_semaphore()
    for k in range(1, slots):
        pl.semaphore_signal(
            barrier, inc=1, device_id={"store": lax.rem(me + k, slots)}, device_id_type=MESH
        )
    for k in range(1, peers):
        pl.semaphore_signal(
            barrier, inc=1, device_id={"mp": lax.rem(part + k, peers)}, device_id_type=MESH
        )
    pl.semaphore_wait(barrier, slots + peers - 2)

    def strip_copy(k):
        to = lax.rem(me + k, slots)
        mine = pl.ds(pl.multiple_of(part * strip, strip), strip)
        return pltpu.make_async_remote_copy(
            src_ref=hidden_ref.at[0, mine, pl.ds(pl.multiple_of(to * depth, depth), depth)],
            dst_ref=tokens.at[me, mine, :],
            send_sem=a_send.at[k],
            recv_sem=a_recv.at[k],
            device_id={"store": to},
            device_id_type=MESH,
        )

    def spread_copy(k, d):
        source = lax.rem(me - k + slots, slots)
        mine = pl.ds(pl.multiple_of(part * strip, strip), strip)
        return pltpu.make_async_remote_copy(
            src_ref=tokens.at[source, mine, :],
            dst_ref=tokens.at[source, mine, :],
            send_sem=b_send.at[k, d],
            recv_sem=b_recv.at[k, d],
            device_id={"mp": lax.rem(part + d, peers)},
            device_id_type=MESH,
        )

    def block_copy(k):
        to = lax.rem(me + k, slots)
        return pltpu.make_async_remote_copy(
            src_ref=sending_ref.at[to],
            dst_ref=blocks.at[me],
            send_sem=k_send.at[k],
            recv_sem=k_recv.at[k],
            device_id={"store": to},
            device_id_type=MESH,
        )

    def sum_copy(s, q, up):
        index = s + 1 if up else s
        return pltpu.make_async_remote_copy(
            src_ref=sums.at[q, s],
            dst_ref=arrived.at[index, q],
            send_sem=p_send.at[index, q],
            recv_sem=p_recv.at[index, q],
            device_id={"store": lax.rem(me + 1, slots) if up else lax.rem(me + slots - 1, slots)},
            device_id_type=MESH,
        )

    def each(count, body, first=0):
        def step(i, carry):
            body(i)
            return carry

        lax.fori_loop(first, count, step, 0)

    each(slots, lambda k: strip_copy(k).start(), 1)
    each(slots, lambda k: block_copy(k).start(), 1)
    tokens[me] = hidden_ref[0, :, pl.ds(pl.multiple_of(me * depth, depth), depth)]

    def spread(k):
        strip_copy(k).wait_recv()
        for d in range(1, peers):
            spread_copy(k, d).start()

    each(slots, spread, 1)

    def spread_wait(k):
        for d in range(1, peers):
            spread_copy(k, d).wait_recv()

    each(slots, spread_wait, 1)
    for load in loads:
        load.wait()

    group = 4 if slots % 4 == 0 else 1

    def project(q, panel):
        def some(i):
            t = tokens[pl.ds(i * group, group)].reshape(group * rows, depth)
            sums[q, pl.ds(i * group, group)] = jnp.dot(
                t, panel, preferred_element_type=jnp.float32
            ).reshape(group, rows, width)

        each(slots // group, some)

    def relay_up(k, q):
        s = slots - 1 - k

        @pl.when(s > me)
        def _():
            @pl.when(me > 0)
            def _():
                sum_copy(s, q, True).wait_recv()
                sums[q, s] = sums[q, s] + arrived[s + 1, q]

            sum_copy(s, q, True).start()

    def relay_down(k, q):
        @pl.when(k < me)
        def _():
            @pl.when(me < slots - 1)
            def _():
                sum_copy(k, q, False).wait_recv()
                sums[q, k] = sums[q, k] + arrived[k, q]

            sum_copy(k, q, False).start()

    for q in range(chunks):
        if q < chunks - 1:
            project(q, wq[:, q * width : (q + 1) * width])
        else:
            project(q, wkv[...])

    def relay(i):
        k, q = i // chunks, i % chunks
        relay_up(k, q)
        relay_down(k, q)

    each((slots - 1) * chunks, relay)

    def settle(q):
        @pl.when(me > 0)
        def _():
            sum_copy(me, q, True).wait_recv()
            sums[q, me] = sums[q, me] + arrived[me + 1, q]

        @pl.when(me < slots - 1)
        def _():
            sum_copy(me, q, False).wait_recv()
            sums[q, me] = sums[q, me] + arrived[me, q]

    each(chunks, settle)

    qc, qs = qc_ref[...], qs_ref[...]
    for g in range(kv_heads):
        at = g * 2 * HD
        keys[g, past:, :] = turn(sums[chunks - 1, me, :, at : at + HD], qc, qs).astype(jnp.bfloat16)
        values[g, past:, :] = sums[chunks - 1, me, :, at + HD : at + 2 * HD].astype(jnp.bfloat16)
    for h in range(heads):
        q, at = divmod(h * HD, width)
        queries[h * rows : (h + 1) * rows, :] = turn(
            sums[q, me, :, at : at + HD], qc, qs
        ).astype(jnp.bfloat16)

    def rotate_share(source):
        at_t = pl.multiple_of(source * share, share)
        tc, ts = tc_ref[pl.ds(at_t, share), :], ts_ref[pl.ds(at_t, share), :]

        def one(c):
            at_k = pl.multiple_of((source * NCH + c) * share, share)
            oc, os = oc_ref[pl.ds(c, 1), :], os_ref[pl.ds(c, 1), :]
            cos = tc * oc - ts * os
            sin = ts * oc + tc * os
            for g in range(kv_heads):
                at = g * 2 * HD
                x = blocks[source, c, :, at : at + HD].astype(jnp.float32)
                keys[g, pl.ds(at_k, share), :] = turn(x, cos, sin).astype(jnp.bfloat16)
                values[g, pl.ds(at_k, share), :] = blocks[source, c, :, at + HD : at + 2 * HD]

        each(NCH, one)

    own_copy.wait()
    rotate_share(me)

    def take(k):
        block_copy(k).wait_recv()
        rotate_share(lax.rem(me - k + slots, slots))

    each(slots, take, 1)

    block = 2 * rows
    steps = heads // 2
    span = 512
    factor = math.log2(math.e) / math.sqrt(HD)
    lower = lax.broadcasted_iota(jnp.int32, (block, rows), 0) % rows >= lax.broadcasted_iota(
        jnp.int32, (block, rows), 1
    )
    contract = (((1,), (1,)), ((), ()))

    def one_block(b):
        g = (b * 2) // sharing
        q = queries[pl.ds(pl.multiple_of(b * block, block), block), :]
        own = lax.dot_general(q, keys[g, past:, :], contract, preferred_element_type=jnp.float32)
        own = jnp.where(lower, own, -jnp.inf)
        top = own
        for j in range(past // span):
            s = lax.dot_general(
                q, keys[g, j * span : (j + 1) * span, :], contract,
                preferred_element_type=jnp.float32,
            )
            scores[:, j * span : (j + 1) * span] = s
            for k in range(span // HD):
                top = jnp.maximum(top, s[:, k * HD : (k + 1) * HD])
        top = jnp.max(top, axis=1, keepdims=True)
        w = jnp.exp2((own - top) * factor)
        total = w
        mixed = jnp.dot(
            w.astype(jnp.bfloat16), values[g, past:, :], preferred_element_type=jnp.float32
        )
        for j in range(past // span):
            w = jnp.exp2((scores[:, j * span : (j + 1) * span] - top) * factor)
            for k in range(span // HD):
                total = total + w[:, k * HD : (k + 1) * HD]
            mixed = mixed + jnp.dot(
                w.astype(jnp.bfloat16), values[g, j * span : (j + 1) * span, :],
                preferred_element_type=jnp.float32,
            )
        done = (mixed / jnp.sum(total, axis=1, keepdims=True)).astype(out_ref.dtype)
        for k in range(2):
            at = pl.multiple_of((b * 2 + k) * HD, HD)
            out_ref[0, :, pl.ds(at, HD)] = done[k * rows : (k + 1) * rows, :]

    each(steps, one_block)

    def drain(k):
        strip_copy(k).wait_send()
        block_copy(k).wait_send()
        for d in range(1, peers):
            spread_copy(k, d).wait_send()

    each(slots, drain, 1)

    def drain_sums(i):
        k, q = i // chunks, i % chunks

        @pl.when(slots - 1 - k > me)
        def _():
            sum_copy(slots - 1 - k, q, True).wait_send()

        @pl.when(k < me)
        def _():
            sum_copy(k, q, False).wait_send()

    each((slots - 1) * chunks, drain_sums)


def per_device(hidden, query_weight, keyvalue_weight, block_store, block_ids, offsets, served):
    slots = lax.axis_size("store")
    peers = lax.axis_size("mp")
    me = lax.axis_index("store")
    rows, model = hidden.shape[1:]
    share, kv_cols = block_store.shape[1:]
    q_cols = query_weight.shape[1]
    heads = q_cols // HD
    kv_heads = kv_cols // (2 * HD)
    chunks = q_cols // kv_cols + 1
    depth = model // slots
    past = NCH * L
    sending = gather_blocks(block_ids, served, block_store)
    qc, qs = signed_tables(past + GAP + np.arange(rows))
    tc, ts = signed_tables(np.arange(L))
    oc, os = offset_tables(offsets[served[me]])
    vmem = pl.BlockSpec(memory_space=pltpu.VMEM)
    hbm = pl.BlockSpec(memory_space=pl.ANY)
    dma = pltpu.SemaphoreType.DMA
    return pl.pallas_call(
        functools.partial(serve_body, slots, peers, heads, kv_heads),
        out_shape=jax.ShapeDtypeStruct((1, rows, q_cols), jnp.bfloat16),
        in_specs=[vmem, hbm, hbm, hbm] + [vmem] * 6,
        out_specs=vmem,
        scratch_shapes=[
            pltpu.VMEM((slots, rows, depth), jnp.bfloat16),
            pltpu.VMEM(query_weight.shape, jnp.bfloat16),
            pltpu.VMEM(keyvalue_weight.shape, jnp.bfloat16),
            pltpu.VMEM((chunks, slots, rows, kv_cols), jnp.float32),
            pltpu.VMEM((slots + 1, chunks, rows, kv_cols), jnp.float32),
            pltpu.VMEM((slots, NCH, share, kv_cols), jnp.bfloat16),
            pltpu.VMEM((kv_heads, past + rows, HD), jnp.bfloat16),
            pltpu.VMEM((kv_heads, past + rows, HD), jnp.bfloat16),
            pltpu.VMEM((heads * rows, HD), jnp.bfloat16),
            pltpu.VMEM((2 * rows, past), jnp.float32),
            dma((2,)),
            dma((1,)),
            dma((slots,)),
            dma((slots,)),
            dma((slots, peers)),
            dma((slots, peers)),
            dma((slots,)),
            dma((slots,)),
            dma((slots + 1, chunks)),
            dma((slots + 1, chunks)),
        ],
        compiler_params=pltpu.CompilerParams(
            vmem_limit_bytes=60 << 20, collective_id=0, has_side_effects=True
        ),
        name="serve",
    )(hidden, query_weight, keyvalue_weight, sending, qc, qs, tc, ts, oc, os)


def solution(mesh):
    in_specs = (
        P(("groups", "store"), None, None),
        P("store", "mp"),
        P("store", "mp"),
        P("groups", "store", "mp"),
        P("groups", None),
        P("groups", None),
        P("groups"),
    )
    out_specs = P(("groups", "store"), None, "mp")
    return jax.shard_map(
        per_device, mesh=mesh, in_specs=in_specs, out_specs=out_specs, check_vma=False
    )
```

time: 305 us -> 221 us (0.72); the launches traced: 300 us -> 220 us
  waiting for transfers between devices: 85.6 us -> 0 us
  Pallas kernels: 150 us -> 213 us
  blocking collectives: 29 us -> 0 us
  between operations: 15.5 us -> 1.96 us
  starting transfers between devices: 6.79 us -> 0 us
  matrix products: 5.23 us -> 0 us
    all_to_all x1 -> x0, waiting for transfers between devices: 85.6 us -> none  [per_device(): lax.all_to_all(sending, 'store', split_axis=0, concat_axis=0, tiled=True)]
    pallas_call x2, Pallas kernels: 150 us -> 213 us  [the longest x1 202 us: per_device(): pl.pallas_call(functools.partial(serve_body, slots, peers, heads, kv_head...]
    all_to_all x1 -> x0, blocking collectives: 29 us -> none  [per_device(): lax.all_to_all(pieces, 'store', split_axis=0, concat_axis=0, tiled=True)]
    all_to_all x1 -> x0, starting transfers between devices: 6.78 us -> none  [per_device(): lax.all_to_all(sending, 'store', split_axis=0, concat_axis=0, tiled=True)]
    dot_general x2 -> x0, matrix products: 5.23 us -> none  [the longest x1 4.52 us: per_device(): jnp.dot(tokens, query_weight, preferred_element_type=jnp.float32)]
  transfers between devices with their start and end apart: 2 -> 0, of which waited for: 1 -> 0; matrix products, arithmetic and copies ran while one was open for 0% -> 0% of each run, Pallas kernels for 43% -> 0%
where the time goes in v2:
time: 221 us; the launch traced here: 220 us
  Pallas kernels  213 us (96%)
  local copies, waits for them, and re-layouts  3.12 us (1%)
    pallas_call x1, Pallas kernels, per_device(): pl.pallas_call(functools.partial(serve_body, slots, peers, heads, kv_head...  202 us
    pallas_call x1, Pallas kernels, gather_blocks(): pl.pallas_call(gather_body, grid_spec=pltpu.PrefetchScalarGridSpec(num_sc...  10.9 us

profile of v2, /device:TPU:10, one launch (start us, length us, event | category | flops | bytes accessed | tf_op | source)
XLA Modules:
  0.0 220.1 jit_solution(8231771838902860236)
XLA Ops:
  0.0 1.2 dynamic_slice.6
  3.2 0.7 convert_bitcast_fusion
  3.9 0.8 fusion.5
  4.7 0.7 pad_maximum_fusion
  5.3 10.9 %gather_blocks.1.sending_ref = bf16[4,4,256,512]{3,2,1,0:T(8,128)(2,1)} custom-call(s32[4,4]{1,0:T(4,128)} %ids_ref.1, s32[4]{0:T(128)} %served_ref.1, bf16[64,256,512]{2,1,0:T(8,128)(2,1)} %store_ref.1), custom_call_target="tpu_custom_call" | custom-call | tf_op jit(solution)/shard_map/gather_blocks/pallas_call | solution.py:51
  16.3 202.0 %serve.1 = bf16[1,128,2048]{2,1,0:T(8,128)(2,1)} custom-call(bf16[1,128,4096]{2,1,0:T(8,128)(2,1)} %hidden_ref.1, bf16[1024,2048]{1,0:T(8,128)(2,1)} %wq_hbm.1, bf16[1024,512]{1,0:T(8,128)(2,1)} %wkv_hbm.1, bf16[4,4,256,512]{3,2,1,0:T(8,128)(2,1)} %gather_blocks.1.sending_ref, f32[128,128]{1,0:T(8,128)} %constant.27.clone.qc_ref, ...), custom_call_target="tpu_custom_call" | custom-call | tf_op jit(solution)/shard_map/serve/pallas_call | solution.py:361
  218.2 1.9 copy.14

commit v3 on v2

--- a/solution.py
+++ b/solution.py
@@ -41,22 +41,33 @@
     return jnp.concatenate([cos, cos], axis=1), jnp.concatenate([-sin, sin], axis=1)
 
 
-def gather_body(ids_ref, served_ref, store_ref, out_ref):
-    out_ref[0] = store_ref[...]
+def gather_body(slots, ids_ref, served_ref, store_ref, out_ref, sems):
+    copies = []
+    for s in range(slots):
+        request = served_ref[s]
+        for c in range(NCH):
+            copy = pltpu.make_async_copy(
+                store_ref.at[ids_ref[request, c]], out_ref.at[s, c], sems.at[s, c]
+            )
+            copy.start()
+            copies.append(copy)
+    for copy in copies:
+        copy.wait()
 
 
 def gather_blocks(block_ids, served, block_store):
     slots = served.shape[0]
-    block = (1,) + block_store.shape[1:]
     return pl.pallas_call(
-        gather_body,
+        functools.partial(gather_body, slots),
         grid_spec=pltpu.PrefetchScalarGridSpec(
             num_scalar_prefetch=2,
-            grid=(slots, NCH),
-            in_specs=[pl.BlockSpec(block, lambda s, c, ids, served: (ids[served[s], c], 0, 0))],
-            out_specs=pl.BlockSpec((1,) + block, lambda s, c, ids, served: (s, c, 0, 0)),
+            grid=(),
+            in_specs=[pl.BlockSpec(memory_space=pl.ANY)],
+            out_specs=pl.BlockSpec(memory_space=pltpu.VMEM),
+            scratch_shapes=[pltpu.SemaphoreType.DMA((slots, NCH))],
         ),
         out_shape=jax.ShapeDtypeStruct((slots, NCH) + block_store.shape[1:], block_store.dtype),
+        compiler_params=pltpu.CompilerParams(vmem_limit_bytes=16 << 20),
         name="gather_blocks",
     )(block_ids, served, block_store)
 
@@ -72,7 +83,7 @@
     slots, peers, heads, kv_heads,
     hidden_ref, wq_hbm, wkv_hbm, sending_ref, qc_ref, qs_ref, tc_ref, ts_ref, oc_ref, os_ref,
     out_ref,
-    tokens, wq, wkv, sums, arrived, blocks, keys, values, queries, scores,
+    tokens, wq, wkv, sums, arrived, blocks, keys, fresh, queries, scores, weights, totals, mixed,
     load_sem, own_sem, a_send, a_recv, b_send, b_recv, k_send, k_recv, p_send, p_recv,
 ):
     me = lax.axis_index("store")
@@ -129,16 +140,25 @@
             device_id_type=MESH,
         )
 
-    def block_copy(k):
+    def block_copy(k, g, v):
         to = lax.rem(me + k, slots)
+        cols = pl.ds(pl.multiple_of((2 * g + v) * HD, HD), HD)
         return pltpu.make_async_remote_copy(
-            src_ref=sending_ref.at[to],
-            dst_ref=blocks.at[me],
-            send_sem=k_send.at[k],
-            recv_sem=k_recv.at[k],
+            src_ref=sending_ref.at[to, :, :, cols],
+            dst_ref=blocks.at[me, :, :, cols],
+            send_sem=k_send.at[k, 2 * g + v],
+            recv_sem=k_recv.at[k, 2 * g + v],
             device_id={"store": to},
             device_id_type=MESH,
         )
+
+    half_pieces = (slots - 1) * kv_heads
+
+    def piece(i):
+        v, r = i // half_pieces, i % half_pieces
+        return block_copy(1 + r // kv_heads, r % kv_heads, v)
+
+    edge = (me == 0) | (me == slots - 1)
 
     def sum_copy(s, q, up):
         index = s + 1 if up else s
@@ -159,7 +179,6 @@
         lax.fori_loop(first, count, step, 0)
 
     each(slots, lambda k: strip_copy(k).start(), 1)
-    each(slots, lambda k: block_copy(k).start(), 1)
     tokens[me] = hidden_ref[0, :, pl.ds(pl.multiple_of(me * depth, depth), depth)]
 
     def spread(k):
@@ -198,7 +217,9 @@
                 sum_copy(s, q, True).wait_recv()
                 sums[q, s] = sums[q, s] + arrived[s + 1, q]
 
-            sum_copy(s, q, True).start()
+            @pl.when((me > 0) | (k > 0))
+            def _():
+                sum_copy(s, q, True).start()
 
     def relay_down(k, q):
         @pl.when(k < me)
@@ -208,7 +229,9 @@
                 sum_copy(k, q, False).wait_recv()
                 sums[q, k] = sums[q, k] + arrived[k, q]
 
-            sum_copy(k, q, False).start()
+            @pl.when((me < slots - 1) | (k > 0))
+            def _():
+                sum_copy(k, q, False).start()
 
     for q in range(chunks):
         if q < chunks - 1:
@@ -216,12 +239,47 @@
         else:
             project(q, wkv[...])
 
+        @pl.when(me == 0)
+        def _():
+            sum_copy(slots - 1, q, True).start()
+
+        @pl.when(me == slots - 1)
+        def _():
+            sum_copy(0, q, False).start()
+
+    steps = (slots - 1) * chunks
+    paced = min(steps, 2 * half_pieces)
+
     def relay(i):
         k, q = i // chunks, i % chunks
         relay_up(k, q)
         relay_down(k, q)
 
-    each((slots - 1) * chunks, relay)
+        @pl.when(jnp.logical_not(edge) & (i < paced))
+        def _():
+            piece(i).start()
+
+    each(steps, relay)
+
+    def drain_sums(i):
+        k, q = i // chunks, i % chunks
+
+        @pl.when(slots - 1 - k > me)
+        def _():
+            sum_copy(slots - 1 - k, q, True).wait_send()
+
+        @pl.when(k < me)
+        def _():
+            sum_copy(k, q, False).wait_send()
+
+    @pl.when(edge)
+    def _():
+        each(steps, drain_sums)
+        each(half_pieces, lambda i: piece(i).start())
+
+    @pl.when(jnp.logical_not(edge))
+    def _():
+        each(2 * half_pieces, lambda i: piece(i).start(), paced)
 
     def settle(q):
         @pl.when(me > 0)
@@ -240,7 +298,7 @@
     for g in range(kv_heads):
         at = g * 2 * HD
         keys[g, past:, :] = turn(sums[chunks - 1, me, :, at : at + HD], qc, qs).astype(jnp.bfloat16)
-        values[g, past:, :] = sums[chunks - 1, me, :, at + HD : at + 2 * HD].astype(jnp.bfloat16)
+        fresh[g] = sums[chunks - 1, me, :, at + HD : at + 2 * HD].astype(jnp.bfloat16)
     for h in range(heads):
         q, at = divmod(h * HD, width)
         queries[h * rows : (h + 1) * rows, :] = turn(
@@ -260,21 +318,25 @@
                 at = g * 2 * HD
                 x = blocks[source, c, :, at : at + HD].astype(jnp.float32)
                 keys[g, pl.ds(at_k, share), :] = turn(x, cos, sin).astype(jnp.bfloat16)
-                values[g, pl.ds(at_k, share), :] = blocks[source, c, :, at + HD : at + 2 * HD]
 
         each(NCH, one)
 
     own_copy.wait()
     rotate_share(me)
 
+    @pl.when(edge)
+    def _():
+        each(half_pieces, lambda i: piece(i).wait_send())
+        each(2 * half_pieces, lambda i: piece(i).start(), half_pieces)
+
     def take(k):
-        block_copy(k).wait_recv()
+        for g in range(kv_heads):
+            block_copy(k, g, 0).wait_recv()
         rotate_share(lax.rem(me - k + slots, slots))
 
     each(slots, take, 1)
 
     block = 2 * rows
-    steps = heads // 2
     span = 512
     factor = math.log2(math.e) / math.sqrt(HD)
     lower = lax.broadcasted_iota(jnp.int32, (block, rows), 0) % rows >= lax.broadcasted_iota(
@@ -282,9 +344,10 @@
     )
     contract = (((1,), (1,)), ((), ()))
 
-    def one_block(b):
+    def weigh(b):
         g = (b * 2) // sharing
-        q = queries[pl.ds(pl.multiple_of(b * block, block), block), :]
+        at = pl.ds(pl.multiple_of(b * block, block), block)
+        q = queries[at, :]
         own = lax.dot_general(q, keys[g, past:, :], contract, preferred_element_type=jnp.float32)
         own = jnp.where(lower, own, -jnp.inf)
         top = own
@@ -299,44 +362,60 @@
         top = jnp.max(top, axis=1, keepdims=True)
         w = jnp.exp2((own - top) * factor)
         total = w
-        mixed = jnp.dot(
-            w.astype(jnp.bfloat16), values[g, past:, :], preferred_element_type=jnp.float32
-        )
+        weights[at, past:] = w.astype(jnp.bfloat16)
         for j in range(past // span):
             w = jnp.exp2((scores[:, j * span : (j + 1) * span] - top) * factor)
             for k in range(span // HD):
                 total = total + w[:, k * HD : (k + 1) * HD]
-            mixed = mixed + jnp.dot(
-                w.astype(jnp.bfloat16), values[g, j * span : (j + 1) * span, :],
-                preferred_element_type=jnp.float32,
-            )
-        done = (mixed / jnp.sum(total, axis=1, keepdims=True)).astype(out_ref.dtype)
-        for k in range(2):
-            at = pl.multiple_of((b * 2 + k) * HD, HD)
-            out_ref[0, :, pl.ds(at, HD)] = done[k * rows : (k + 1) * rows, :]
-
-    each(steps, one_block)
+            weights[at, j * span : (j + 1) * span] = w.astype(jnp.bfloat16)
+        totals[at, :] = total
+
+    each(heads // 2, weigh)
+
+    stack = sharing * rows
+    some = NCH * share
+
+    def mix(source, first):
+        cols = pl.ds(pl.multiple_of(source * some, some), some)
+        for g in range(kv_heads):
+            at = slice(g * stack, (g + 1) * stack)
+            v = blocks[source, :, :, (2 * g + 1) * HD : (2 * g + 2) * HD].reshape(some, HD)
+            term = jnp.dot(weights[at, cols], v, preferred_element_type=jnp.float32)
+            if first:
+                mixed[at, :] = term + jnp.dot(
+                    weights[at, past:], fresh[g], preferred_element_type=jnp.float32
+                )
+            else:
+                mixed[at, :] = mixed[at, :] + term
+
+    mix(me, True)
+
+    def take_values(k):
+        for g in range(kv_heads):
+            block_copy(k, g, 1).wait_recv()
+        mix(lax.rem(me - k + slots, slots), False)
+
+    each(slots, take_values, 1)
+
+    def finish(h):
+        at = pl.ds(pl.multiple_of(h * rows, rows), rows)
+        done = mixed[at, :] / jnp.sum(totals[at, :], axis=1, keepdims=True)
+        out_ref[0, :, pl.ds(pl.multiple_of(h * HD, HD), HD)] = done.astype(out_ref.dtype)
+
+    each(heads, finish)
 
     def drain(k):
         strip_copy(k).wait_send()
-        block_copy(k).wait_send()
         for d in range(1, peers):
             spread_copy(k, d).wait_send()
 
     each(slots, drain, 1)
-
-    def drain_sums(i):
-        k, q = i // chunks, i % chunks
-
-        @pl.when(slots - 1 - k > me)
-        def _():
-            sum_copy(slots - 1 - k, q, True).wait_send()
-
-        @pl.when(k < me)
-        def _():
-            sum_copy(k, q, False).wait_send()
-
-    each((slots - 1) * chunks, drain_sums)
+    each(2 * half_pieces, lambda i: piece(i).wait_send(), half_pieces)
+
+    @pl.when(jnp.logical_not(edge))
+    def _():
+        each(steps, drain_sums)
+        each(half_pieces, lambda i: piece(i).wait_send())
 
 
 def per_device(hidden, query_weight, keyvalue_weight, block_store, block_ids, offsets, served):
@@ -371,22 +450,25 @@
             pltpu.VMEM((slots + 1, chunks, rows, kv_cols), jnp.float32),
             pltpu.VMEM((slots, NCH, share, kv_cols), jnp.bfloat16),
             pltpu.VMEM((kv_heads, past + rows, HD), jnp.bfloat16),
-            pltpu.VMEM((kv_heads, past + rows, HD), jnp.bfloat16),
+            pltpu.VMEM((kv_heads, rows, HD), jnp.bfloat16),
             pltpu.VMEM((heads * rows, HD), jnp.bfloat16),
             pltpu.VMEM((2 * rows, past), jnp.float32),
+            pltpu.VMEM((heads * rows, past + rows), jnp.bfloat16),
+            pltpu.VMEM((heads * rows, HD), jnp.float32),
+            pltpu.VMEM((heads * rows, HD), jnp.float32),
             dma((2,)),
             dma((1,)),
             dma((slots,)),
             dma((slots,)),
             dma((slots, peers)),
             dma((slots, peers)),
-            dma((slots,)),
-            dma((slots,)),
+            dma((slots, 2 * kv_heads)),
+            dma((slots, 2 * kv_heads)),
             dma((slots + 1, chunks)),
             dma((slots + 1, chunks)),
         ],
         compiler_params=pltpu.CompilerParams(
-            vmem_limit_bytes=60 << 20, collective_id=0, has_side_effects=True
+            vmem_limit_bytes=63 << 20, collective_id=0, has_side_effects=True
         ),
         name="serve",
     )(hidden, query_weight, keyvalue_weight, sending, qc, qs, tc, ts, oc, os)

time: 221 us -> 237 us (1.072)
  local copies, waits for them, and re-layouts: 3.12 us -> 12.1 us
  Pallas kernels: 213 us -> 220 us
    pallas_call x1, Pallas kernels: 202 us -> 219 us  [per_device(): pl.pallas_call(functools.partial(serve_body, slots, peers, heads, kv_head...]
    pallas_call x1, Pallas kernels: 10.9 us -> 1.11 us  [gather_blocks(): pl.pallas_call(functools.partial(gather_body, slots), grid_spec=pltpu.Pre...]
    unnamed x1 -> x9, local copies, waits for them, and re-layouts: 1.88 us -> 10.9 us
where the time goes in v3:
time: 237 us; the launch traced here: 236 us
  Pallas kernels  220 us (93%)
  local copies, waits for them, and re-layouts  12.1 us (5%)
    pallas_call x1, Pallas kernels, per_device(): pl.pallas_call(functools.partial(serve_body, slots, peers, heads, kv_head...  219 us
    unnamed x9, local copies, waits for them, and re-layouts  10.9 us

profile of v3, /device:TPU:10, one launch (start us, length us, event | category | flops | bytes accessed | tf_op | source)
XLA Modules:
  0.0 236.4 jit_solution(5270587822489025054)
XLA Ops:
  0.0 1.2 dynamic_slice.6
  3.2 0.7 convert_bitcast_fusion
  3.9 0.8 fusion.5
  4.7 0.7 pad_maximum_fusion
  5.3 0.0 copy-start.1
  5.3 5.8 %copy-done.1 = bf16[64,256,512]{2,1,0:T(8,128)(2,1)S(1)} copy-done((bf16[64,256,512]{2,1,0:T(8,128)(2,1)S(1)}, bf16[64,256,512]{2,1,0:T(8,128)(2,1)}, u32[]{:S(2)}) %copy-start.1) | copy-done | bytes 16777240
  11.1 0.0 copy-start.2
  11.1 0.7 copy-done.2
  11.8 0.0 copy-start.3
  11.8 0.7 copy-done.3
  12.4 1.1 gather_blocks.1.sending_ref
  13.5 0.0 copy-start
  13.6 1.9 copy-done
  15.5 219.1 %serve.1 = bf16[1,128,2048]{2,1,0:T(8,128)(2,1)} custom-call(bf16[1,128,4096]{2,1,0:T(8,128)(2,1)} %hidden_ref.1, bf16[1024,2048]{1,0:T(8,128)(2,1)} %wq_hbm.1, bf16[1024,512]{1,0:T(8,128)(2,1)} %wkv_hbm.1, bf16[4,4,256,512]{3,2,1,0:T(8,128)(2,1)} %copy-done, f32[128,128]{1,0:T(8,128)} %constant.27.clone.qc_ref, f32[128,128]{1,0:T(8,128)} %constant.28.clone.qs_ref, ...), custom_call_target="tpu_custom_call" | custom-call | tf_op jit(solution)/shard_map/serve/pallas_call | solution.py:440
  234.6 1.9 copy.14
Async XLA Ops:
  5.3 5.8 %copy-start.1 = (bf16[64,256,512]{2,1,0:T(8,128)(2,1)S(1)}, bf16[64,256,512]{2,1,0:T(8,128)(2,1)}, u32[]{:S(2)}) copy-start(bf16[64,256,512]{2,1,0:T(8,128)(2,1)} %store_ref.1) | copy-start | bytes 50331652
  11.1 0.7 copy-start.2
  11.8 0.7 copy-start.3
  13.5 1.9 copy-start

commit v4 on v3

--- a/solution.py
+++ b/solution.py
@@ -67,7 +67,7 @@
             scratch_shapes=[pltpu.SemaphoreType.DMA((slots, NCH))],
         ),
         out_shape=jax.ShapeDtypeStruct((slots, NCH) + block_store.shape[1:], block_store.dtype),
-        compiler_params=pltpu.CompilerParams(vmem_limit_bytes=16 << 20),
+        compiler_params=pltpu.CompilerParams(vmem_limit_bytes=56 << 20),
         name="gather_blocks",
     )(block_ids, served, block_store)
 
@@ -77,6 +77,7 @@
 
 
 MESH = pl.DeviceIdType.MESH
+ENDS, MIDDLE = 2, 2
 
 
 def serve_body(
@@ -179,6 +180,16 @@
         lax.fori_loop(first, count, step, 0)
 
     each(slots, lambda k: strip_copy(k).start(), 1)
+    ends_first, middle_first = ENDS * half_pieces, MIDDLE * half_pieces
+
+    @pl.when(edge)
+    def _():
+        each(ends_first, lambda i: piece(i).start())
+
+    @pl.when(jnp.logical_not(edge))
+    def _():
+        each(middle_first, lambda i: piece(i).start())
+
     tokens[me] = hidden_ref[0, :, pl.ds(pl.multiple_of(me * depth, depth), depth)]
 
     def spread(k):
@@ -255,9 +266,9 @@
         relay_up(k, q)
         relay_down(k, q)
 
-        @pl.when(jnp.logical_not(edge) & (i < paced))
-        def _():
-            piece(i).start()
+        @pl.when(jnp.logical_not(edge) & (i + middle_first < paced))
+        def _():
+            piece(i + middle_first).start()
 
     each(steps, relay)
 
@@ -274,8 +285,7 @@
 
     @pl.when(edge)
     def _():
-        each(steps, drain_sums)
-        each(half_pieces, lambda i: piece(i).start())
+        each(2 * half_pieces, lambda i: piece(i).start(), ends_first)
 
     @pl.when(jnp.logical_not(edge))
     def _():
@@ -323,11 +333,6 @@
 
     own_copy.wait()
     rotate_share(me)
-
-    @pl.when(edge)
-    def _():
-        each(half_pieces, lambda i: piece(i).wait_send())
-        each(2 * half_pieces, lambda i: piece(i).start(), half_pieces)
 
     def take(k):
         for g in range(kv_heads):
@@ -410,12 +415,8 @@
             spread_copy(k, d).wait_send()
 
     each(slots, drain, 1)
-    each(2 * half_pieces, lambda i: piece(i).wait_send(), half_pieces)
-
-    @pl.when(jnp.logical_not(edge))
-    def _():
-        each(steps, drain_sums)
-        each(half_pieces, lambda i: piece(i).wait_send())
+    each(2 * half_pieces, lambda i: piece(i).wait_send())
+    each(steps, drain_sums)
 
 
 def per_device(hidden, query_weight, keyvalue_weight, block_store, block_ids, offsets, served):

time: 237 us -> 217 us (0.916)
  Pallas kernels: 220 us -> 210 us
  local copies, waits for them, and re-layouts: 12.1 us -> 3.12 us
    pallas_call x1, Pallas kernels: 219 us -> 205 us  [per_device(): pl.pallas_call(functools.partial(serve_body, slots, peers, heads, kv_head...]
    unnamed x9 -> x1, local copies, waits for them, and re-layouts: 10.9 us -> 1.88 us
    pallas_call x1, Pallas kernels: 1.11 us -> 4.91 us  [gather_blocks(): pl.pallas_call(functools.partial(gather_body, slots), grid_spec=pltpu.Pre...]
where the time goes in v4:
time: 217 us
  Pallas kernels  210 us (97%)
  local copies, waits for them, and re-layouts  3.12 us (1%)
    pallas_call x1, Pallas kernels, per_device(): pl.pallas_call(functools.partial(serve_body, slots, peers, heads, kv_head...  205 us
    pallas_call x1, Pallas kernels, gather_blocks(): pl.pallas_call(functools.partial(gather_body, slots), grid_spec=pltpu.Pre...  4.91 us

profile of v4, /device:TPU:10, one launch (start us, length us, event | category | flops | bytes accessed | tf_op | source)
XLA Modules:
  0.0 216.8 jit_solution(17507428049277769983)
XLA Ops:
  0.0 1.2 dynamic_slice.6
  3.2 0.7 convert_bitcast_fusion
  3.9 0.8 fusion.5
  4.7 0.7 pad_maximum_fusion
  5.3 4.9 %gather_blocks.1.sending_ref = bf16[4,4,256,512]{3,2,1,0:T(8,128)(2,1)} custom-call(s32[4,4]{1,0:T(4,128)} %ids_ref.1, s32[4]{0:T(128)} %served_ref.1, bf16[64,256,512]{2,1,0:T(8,128)(2,1)} %store_ref.1), custom_call_target="tpu_custom_call" | custom-call | tf_op jit(solution)/shard_map/gather_blocks/pallas_call | solution.py:60
  10.3 204.6 %serve.1 = bf16[1,128,2048]{2,1,0:T(8,128)(2,1)} custom-call(bf16[1,128,4096]{2,1,0:T(8,128)(2,1)} %hidden_ref.1, bf16[1024,2048]{1,0:T(8,128)(2,1)} %wq_hbm.1, bf16[1024,512]{1,0:T(8,128)(2,1)} %wkv_hbm.1, bf16[4,4,256,512]{3,2,1,0:T(8,128)(2,1)} %gather_blocks.1.sending_ref, f32[128,128]{1,0:T(8,128)} %constant.27.clone.qc_ref, ...), custom_call_target="tpu_custom_call" | custom-call | tf_op jit(solution)/shard_map/serve/pallas_call | solution.py:441
  214.9 1.9 copy.14
